TPU v7x, 128 devices: a whole 4x4x4 slice. The times are simulated.
128 devices in a mesh: dp: 8 (over y, x_lo), mp: 16 (over x_hi, z, core).
Axes of the slice: x: 4 (x_hi: 2, x_lo: 2; x = x_hi * 2 + x_lo), y: 4, z: 4, core: 2. Of those that a mesh axis runs over, the one named last changes fastest.
Arguments:
- hidden_states: bfloat16 [4096, 4096], P('dp', 'mp'), may hold values from -6 to 6
- gate_online: bfloat16 [4096, 14336], P('dp', 'mp'), may hold values from -0.09375 to 0.09375
- up_online: bfloat16 [4096, 14336], P('dp', 'mp'), may hold values from -0.09375 to 0.09375
- down_online: bfloat16 [14336, 4096], P('mp', 'dp'), may hold values from -0.046875 to 0.046875
- gate_previous: bfloat16 [4096, 14336], P(None, 'mp'), may hold values from -0.09375 to 0.09375
- up_previous: bfloat16 [4096, 14336], P(None, 'mp'), may hold values from -0.09375 to 0.09375
- down_previous: bfloat16 [14336, 4096], P('mp'), may hold values from -0.046875 to 0.046875
Outputs:
- online_output: bfloat16 [4096, 4096], P('dp', 'mp')
- target_output: bfloat16 [4096, 4096], P('dp', 'mp')
All inputs are finite; a program needn't handle non-finite values.
Results may differ from a plain program's by a relative error of at most 0.0072.
Values may be sent and summed in bfloat16 or wider, within the bound.
A program may use at most 128 MiB of HBM per device.

v0:
```python
import jax
import jax.numpy as jnp
from jax import lax
from jax.sharding import PartitionSpec as P

POLYAK = 0.25


def blend(online, previous):
    return (
        POLYAK * online.astype(jnp.float32) + (1.0 - POLYAK) * previous.astype(jnp.float32)
    ).astype(jnp.bfloat16)


def add_pair(features_all, piece, previous):
    target_piece = blend(piece, previous)
    online_sum = jnp.dot(features_all, piece, preferred_element_type=jnp.float32)
    target_sum = jnp.dot(features_all, target_piece, preferred_element_type=jnp.float32)
    return (online_sum, target_sum)


def local(
    hidden_states, gate_online, up_online, down_online, gate_previous, up_previous, down_previous
):
    features_all = lax.all_gather(hidden_states, "mp", axis=1, tiled=True)
    gate_o, gate_t = add_pair(
        features_all, lax.all_gather(gate_online, "dp", axis=0, tiled=True), gate_previous
    )
    up_o, up_t = add_pair(
        features_all, lax.all_gather(up_online, "dp", axis=0, tiled=True), up_previous
    )
    inner_o = (jax.nn.silu(gate_o) * up_o).astype(jnp.bfloat16)
    inner_t = (jax.nn.silu(gate_t) * up_t).astype(jnp.bfloat16)
    piece = lax.all_gather(down_online, "dp", axis=1, tiled=True)
    target_piece = blend(piece, down_previous)
    online_part = jnp.dot(inner_o, piece, preferred_element_type=jnp.float32)
    target_part = jnp.dot(inner_t, target_piece, preferred_element_type=jnp.float32)
    terms = jnp.stack([online_part, target_part], axis=0)
    summed = lax.psum_scatter(terms, "mp", scatter_dimension=2, tiled=True)
    result = summed.astype(jnp.bfloat16)
    return (result[0], result[1])


def solution(mesh):
    in_specs = (
        P("dp", "mp"),
        P("dp", "mp"),
        P("dp", "mp"),
        P("mp", "dp"),
        P(None, "mp"),
        P(None, "mp"),
        P("mp", None),
    )
    out_specs = (P("dp", "mp"), P("dp", "mp"))
    return jax.shard_map(local, mesh=mesh, in_specs=in_specs, out_specs=out_specs, check_vma=False)
```

profile of v0, /device:TPU:1, one launch (start us, length us, event | category | flops | bytes accessed | tf_op | source)
XLA Modules:
  0.0 729.1 jit_solution(7389197562212726520)
XLA Ops:
  7.2 0.0 all-gather.5.cloned.1.call-start
  7.2 0.7 all-gather.5.cloned.1.call-update
  7.9 0.0 all-gather.7.cloned.1.call-start
  7.9 0.7 all-gather.7.cloned.1.call-update
  8.6 0.0 all-gather.9.cloned.1.call-start
  8.7 0.7 all-gather.9.cloned.1.call-update
  9.4 0.0 all-gather.11.cloned.1.call-start
  9.4 0.5 all-gather.11.cloned.1.call-update
  10.0 0.0 reduce-scatter.2.cloned.1.call-start
  10.0 60.8 %all-gather.5.cloned.1.call-done = bf16[512,4096]{1,0:T(8,128)(2,1)} async-done(((bf16[512,256]{1,0:T(8,128)(2,1)}), bf16[512,4096]{1,0:T(8,128)(2,1)}) %all-gather.5.cloned.1.call-update) | async-done | bytes 4194320 | tf_op jit(solution)/shard_map/all_gather | solution.py:25
  70.8 147.5 %all-gather.7.cloned.1.call-done = bf16[4096,896]{1,0:T(8,128)(2,1)} async-done(((bf16[512,896]{1,0:T(8,128)(2,1)}), bf16[4096,896]{1,0:T(8,128)(2,1)}) %all-gather.7.cloned.1.call-update) | async-done | bytes 7340048 | tf_op jit(solution)/shard_map/all_gather | solution.py:27
  218.3 0.0 copy-start
  218.3 0.0 copy-start.1
  218.3 10.2 %fusion.22 = f32[512,896]{1,0:T(8,128)} fusion(bf16[512,4096]{1,0:T(8,128)(2,1)} %all-gather.5.cloned.1.call-done, bf16[4096,896]{1,0:T(8,128)(2,1)} %all-gather.7.cloned.1.call-done), kind=kOutput, calls=%fused_computation.31 | convolution fusion | flops 3758096384 | bytes 13369344 | tf_op jit(solution)/shard_map/dot_general | solution.py:17
  228.5 0.0 copy-done
  228.5 0.0 copy-done.1
  228.5 7.9 %fusion = f32[896,512]{0,1:T(8,128)S(1)} fusion(bf16[512,4096]{1,0:T(8,128)(2,1)S(1)} %copy-done.1, bf16[4096,896]{1,0:T(8,128)(2,1)} %param.11, bf16[4096,896]{1,0:T(8,128)(2,1)S(1)} %copy-done), kind=kOutput, calls=%fused_computation.4 | convolution fusion | flops 3780116480 | bytes 20709376 | tf_op jit(solution)/shard_map/dot_general | solution.py:18
  236.5 133.2 %all-gather.9.cloned.1.call-done = bf16[4096,896]{1,0:T(8,128)(2,1)} async-done(((bf16[512,896]{1,0:T(8,128)(2,1)}), bf16[4096,896]{1,0:T(8,128)(2,1)}) %all-gather.9.cloned.1.call-update) | async-done | bytes 7340048 | tf_op jit(solution)/shard_map/all_gather | solution.py:30
  369.7 151.2 %all-gather.11.cloned.1.call-done = bf16[896,4096]{1,0:T(8,128)(2,1)} async-done(((bf16[896,512]{1,0:T(8,128)(2,1)}), bf16[896,4096]{1,0:T(8,128)(2,1)}) %all-gather.11.cloned.1.call-update) | async-done | bytes 7340048 | tf_op jit(solution)/shard_map/all_gather | solution.py:34
  520.9 17.2 %convolution_bitcast_fusion = f32[1,512,4096]{2,1,0:T(8,128)} fusion(bf16[896,4096]{1,0:T(8,128)(2,1)} %all-gather.11.cloned.1.call-done, f32[512,896]{1,0:T(8,128)} %fusion.22, bf16[512,4096]{1,0:T(8,128)(2,1)} %all-gather.5.cloned.1.call-done, bf16[4096,896]{1,0:T(8,128)(2,1)} %all-gather.9.cloned.1.call-done), kind=kOutput, calls=%fused_computation.14 | convolution fusion | flops 7518945280 | bytes 29097984 | tf_op jit(solution)/shard_map/dot_general | solution.py:36
  538.2 22.9 %fusion.9 = f32[1,512,4096]{2,1,0:T(8,128)} fusion(bf16[896,4096]{1,0:T(8,128)(2,1)} %param.13, bf16[896,4096]{1,0:T(8,128)(2,1)} %all-gather.11.cloned.1.call-done, f32[896,512]{0,1:T(8,128)S(1)} %fusion, bf16[512,4096]{1,0:T(8,128)(2,1)} %all-gather.5.cloned.1.call-done, bf16[4096,896]{1,0:T(8,128)(2,1)} %param.12, ...), kind=kOutput, calls=%fused_computation.13 | convolution fusion | flops 7562985472 | bytes 43778048 | tf_op jit(solution)/shard_map/dot_general | solution.py:37
  561.0 11.6 %pad_maximum_fusion = f32[2,512,4096]{2,1,0:T(8,128)} fusion(f32[1,512,4096]{2,1,0:T(8,128)} %fusion.9, f32[1,512,4096]{2,1,0:T(8,128)} %convolution_bitcast_fusion), kind=kLoop, calls=%fused_computation | loop fusion | flops 4194304 | bytes 33554432 | tf_op jit(solution)/shard_map/stack | solution.py:38
  572.6 0.0 reduce-scatter.2.cloned.1.call-update
  572.6 147.9 %reduce-scatter.2.cloned.1.call-done = f32[2,512,256]{2,1,0:T(8,128)} async-done(((f32[2,512,4096]{2,1,0:T(8,128)}), f32[2,512,256]{2,1,0:T(8,128)}) %reduce-scatter.2.cloned.1.call-update) | async-done | bytes 1048592 | tf_op jit(solution)/shard_map/reduce_scatter | solution.py:39
  720.5 1.3 convert_element_type.47
  721.8 0.8 slice_bitcast_fusion
Async XLA Ops:
  7.2 63.6 %all-gather.5.cloned.1.call-start = ((), (), s32[]{:S(2)}) async-start(), calls=%async_computation.1 | async-start | bytes 4456448 | tf_op jit(solution)/shard_map/all_gather | solution.py:25
  7.9 210.4 %all-gather.7.cloned.1.call-start = ((), (), s32[]{:S(2)}) async-start(), calls=%async_computation.2 | async-start | bytes 8257536 | tf_op jit(solution)/shard_map/all_gather | solution.py:27
  8.6 361.0 %all-gather.9.cloned.1.call-start = ((), (), s32[]{:S(2)}) async-start(), calls=%async_computation.3 | async-start | bytes 8257536 | tf_op jit(solution)/shard_map/all_gather | solution.py:30
  9.4 511.5 %all-gather.11.cloned.1.call-start = ((), (), s32[]{:S(2)}) async-start(), calls=%async_computation.4 | async-start | bytes 8257536 | tf_op jit(solution)/shard_map/all_gather | solution.py:34
  10.0 710.6 %reduce-scatter.2.cloned.1.call-start = ((), (), s32[]{:S(2)}) async-start(), calls=%async_computation.5 | async-start | bytes 17825792 | tf_op jit(solution)/shard_map/reduce_scatter | solution.py:39
  218.3 10.2 %copy-start = (bf16[4096,896]{1,0:T(8,128)(2,1)S(1)}, bf16[4096,896]{1,0:T(8,128)(2,1)}, u32[]{:S(2)}) copy-start(bf16[4096,896]{1,0:T(8,128)(2,1)} %all-gather.7.cloned.1.call-done) | copy-start | bytes 22020100
  218.3 10.2 %copy-start.1 = (bf16[512,4096]{1,0:T(8,128)(2,1)S(1)}, bf16[512,4096]{1,0:T(8,128)(2,1)}, u32[]{:S(2)}) copy-start(bf16[512,4096]{1,0:T(8,128)(2,1)} %all-gather.5.cloned.1.call-done) | copy-start | bytes 12582916
Sparse Core Ops, SparseCore 0:
  10.3 60.4 all-gather.4
  72.4 145.8 all-gather.6
  220.0 149.6 all-gather.8
  371.2 149.6 all-gather.10
  572.7 147.7 reduce-scatter.1
where the time goes:
time: 729 us
  waiting for transfers between devices  643 us (88%)
  matrix products  58.3 us (8%)
  between operations  13.8 us (2%)
  other arithmetic  12.8 us (2%)
    all_gather x1, waiting for transfers between devices, local(): piece = lax.all_gather(down_online, 'dp', axis=1, tiled=True)  151 us
    reduce_scatter x1, waiting for transfers between devices, local(): summed = lax.psum_scatter(terms, 'mp', scatter_dimension=2, tiled=True)  148 us
    all_gather x1, waiting for transfers between devices, local(): lax.all_gather(gate_online, 'dp', axis=0, tiled=True)  148 us
    all_gather x1, waiting for transfers between devices, local(): lax.all_gather(up_online, 'dp', axis=0, tiled=True)  133 us
    all_gather x1, waiting for transfers between devices, local(): features_all = lax.all_gather(hidden_states, 'mp', axis=1, tiled=True)  60.8 us
    dot_general x1, matrix products, local(): jnp.dot(inner_t, target_piece, preferred_element_type=jnp.float32)  22.9 us
    dot_general x1, matrix products, local(): online_part = jnp.dot(inner_o, piece, preferred_element_type=jnp.float32)  17.2 us
  transfers between devices with their start and end apart: 5, of which 5 were waited for; matrix products, arithmetic and copies ran while one was open for 2% of the time, Pallas kernels for 0%

commit v1 on v0

--- a/solution.py
+++ b/solution.py
@@ -2,8 +2,18 @@
 import jax.numpy as jnp
 from jax import lax
 from jax.sharding import PartitionSpec as P
+from jax.lax import all_to_all, axis_size
 
 POLYAK = 0.25
+
+
+def update_vector(z):
+    return jnp.concatenate(
+        all_to_all(
+            jnp.stack(axis_size("dp") * [z], axis=0), axis_name="dp", split_axis=0, concat_axis=0
+        ),
+        axis=0,
+    )
 
 
 def blend(online, previous):
@@ -26,9 +36,7 @@
     gate_o, gate_t = add_pair(
         features_all, lax.all_gather(gate_online, "dp", axis=0, tiled=True), gate_previous
     )
-    up_o, up_t = add_pair(
-        features_all, lax.all_gather(up_online, "dp", axis=0, tiled=True), up_previous
-    )
+    up_o, up_t = add_pair(features_all, update_vector(up_online), up_previous)
     inner_o = (jax.nn.silu(gate_o) * up_o).astype(jnp.bfloat16)
     inner_t = (jax.nn.silu(gate_t) * up_t).astype(jnp.bfloat16)
     piece = lax.all_gather(down_online, "dp", axis=1, tiled=True)

time: 729 us -> 616 us (0.84)
  waiting for transfers between devices: 643 us -> 518 us
    all_gather x1 -> x0, waiting for transfers between devices: 133 us -> none  [local(): lax.all_gather(up_online, 'dp', axis=0, tiled=True)]
    all_gather x1, waiting for transfers between devices: 148 us -> 170 us  [local(): lax.all_gather(gate_online, 'dp', axis=0, tiled=True)]
    all_gather x1, waiting for transfers between devices: 151 us -> 134 us  [local(): piece = lax.all_gather(down_online, 'dp', axis=1, tiled=True)]
  transfers between devices with their start and end apart: 5 -> 5, of which waited for: 5 -> 4; matrix products, arithmetic and copies ran while one was open for 2% -> 4% of each run, Pallas kernels for 0% -> 0%
where the time goes in v1:
time: 616 us; the launch traced here: 615 us
  waiting for transfers between devices  518 us (84%)
  matrix products  58.3 us (9%)
  between operations  13.8 us (2%)
  other arithmetic  12.8 us (2%)
    all_gather x1, waiting for transfers between devices, local(): lax.all_gather(gate_online, 'dp', axis=0, tiled=True)  170 us
    reduce_scatter x1, waiting for transfers between devices, local(): summed = lax.psum_scatter(terms, 'mp', scatter_dimension=2, tiled=True)  148 us
    all_gather x1, waiting for transfers between devices, local(): piece = lax.all_gather(down_online, 'dp', axis=1, tiled=True)  134 us
    all_gather x1, waiting for transfers between devices, local(): features_all = lax.all_gather(hidden_states, 'mp', axis=1, tiled=True)  64.9 us
    dot_general x1, matrix products, local(): jnp.dot(inner_t, target_piece, preferred_element_type=jnp.float32)  22.9 us
    dot_general x1, matrix products, local(): online_part = jnp.dot(inner_o, piece, preferred_element_type=jnp.float32)  17.2 us
  transfers between devices with their start and end apart: 5, of which 4 were waited for; matrix products, arithmetic and copies ran while one was open for 4% of the time, Pallas kernels for 0%

profile of v1, /device:TPU:1, one launch (start us, length us, event | category | flops | bytes accessed | tf_op | source)
XLA Modules:
  0.0 615.3 jit_solution(2265880455330164687)
XLA Ops:
  7.2 0.0 all-gather.4.cloned.1.call-start
  7.2 0.7 all-gather.4.cloned.1.call-update
  7.9 0.0 all-gather.6.cloned.1.call-start
  7.9 0.7 all-gather.6.cloned.1.call-update
  8.6 0.0 all-gather.8.cloned.1.call-start
  8.7 0.7 all-gather.8.cloned.1.call-update
  9.4 5.0 stack.8
  14.4 5.9 all-to-all-start
  20.4 0.0 reduce-scatter.2.cloned.1.call-start
  20.4 64.9 %all-gather.4.cloned.1.call-done = bf16[512,4096]{1,0:T(8,128)(2,1)} async-done(((bf16[512,256]{1,0:T(8,128)(2,1)}), bf16[512,4096]{1,0:T(8,128)(2,1)}) %all-gather.4.cloned.1.call-update) | async-done | bytes 4194320 | tf_op jit(solution)/shard_map/all_gather | solution.py:35
  85.3 169.6 %all-gather.6.cloned.1.call-done = bf16[4096,896]{1,0:T(8,128)(2,1)} async-done(((bf16[512,896]{1,0:T(8,128)(2,1)}), bf16[4096,896]{1,0:T(8,128)(2,1)}) %all-gather.6.cloned.1.call-update) | async-done | bytes 7340048 | tf_op jit(solution)/shard_map/all_gather | solution.py:37
  255.0 0.0 copy-start
  255.0 0.0 copy-start.1
  255.0 10.2 %fusion.22 = f32[512,896]{1,0:T(8,128)} fusion(bf16[512,4096]{1,0:T(8,128)(2,1)} %all-gather.4.cloned.1.call-done, bf16[4096,896]{1,0:T(8,128)(2,1)} %all-gather.6.cloned.1.call-done), kind=kOutput, calls=%fused_computation.31 | convolution fusion | flops 3758096384 | bytes 13369344 | tf_op jit(solution)/shard_map/dot_general | solution.py:27
  265.2 0.0 copy-done
  265.2 0.0 copy-done.1
  265.2 7.9 %fusion = f32[896,512]{0,1:T(8,128)S(1)} fusion(bf16[512,4096]{1,0:T(8,128)(2,1)S(1)} %copy-done.1, bf16[4096,896]{1,0:T(8,128)(2,1)} %param.11, bf16[4096,896]{1,0:T(8,128)(2,1)S(1)} %copy-done), kind=kOutput, calls=%fused_computation.4 | convolution fusion | flops 3780116480 | bytes 20709376 | tf_op jit(solution)/shard_map/dot_general | solution.py:28
  273.2 0.0 all-to-all-done
  273.2 133.5 %all-gather.8.cloned.1.call-done = bf16[896,4096]{1,0:T(8,128)(2,1)} async-done(((bf16[896,512]{1,0:T(8,128)(2,1)}), bf16[896,4096]{1,0:T(8,128)(2,1)}) %all-gather.8.cloned.1.call-update) | async-done | bytes 7340048 | tf_op jit(solution)/shard_map/all_gather | solution.py:42
  406.7 17.2 %convolution_bitcast_fusion = f32[1,512,4096]{2,1,0:T(8,128)} fusion(bf16[896,4096]{1,0:T(8,128)(2,1)} %all-gather.8.cloned.1.call-done, f32[512,896]{1,0:T(8,128)} %fusion.22, bf16[512,4096]{1,0:T(8,128)(2,1)} %all-gather.4.cloned.1.call-done, bf16[4096,896]{1,0:T(8,128)(2,1)} %bitcast), kind=kOutput, calls=%fused_computation.14 | convolution fusion | flops 7518945280 | bytes 29097984 | tf_op jit(solution)/shard_map/dot_general | solution.py:44
  424.0 22.9 %fusion.9 = f32[1,512,4096]{2,1,0:T(8,128)} fusion(bf16[896,4096]{1,0:T(8,128)(2,1)} %param.13, bf16[896,4096]{1,0:T(8,128)(2,1)} %all-gather.8.cloned.1.call-done, f32[896,512]{0,1:T(8,128)S(1)} %fusion, bf16[512,4096]{1,0:T(8,128)(2,1)} %all-gather.4.cloned.1.call-done, bf16[4096,896]{1,0:T(8,128)(2,1)} %param.12, bf16[4096,896]{1,0:T(8,128)(2,1)} %bitcast), kind=kOutput, calls=%fused_computation.13 | convolution fusion | flops 7562985472 | bytes 43778048 | tf_op jit(solution)/shard_map/dot_general | solution.py:45
  446.8 11.6 %pad_maximum_fusion = f32[2,512,4096]{2,1,0:T(8,128)} fusion(f32[1,512,4096]{2,1,0:T(8,128)} %fusion.9, f32[1,512,4096]{2,1,0:T(8,128)} %convolution_bitcast_fusion), kind=kLoop, calls=%fused_computation | loop fusion | flops 4194304 | bytes 33554432 | tf_op jit(solution)/shard_map/stack | solution.py:46
  458.4 0.0 reduce-scatter.2.cloned.1.call-update
  458.4 148.3 %reduce-scatter.2.cloned.1.call-done = f32[2,512,256]{2,1,0:T(8,128)} async-done(((f32[2,512,4096]{2,1,0:T(8,128)}), f32[2,512,256]{2,1,0:T(8,128)}) %reduce-scatter.2.cloned.1.call-update) | async-done | bytes 1048592 | tf_op jit(solution)/shard_map/reduce_scatter | solution.py:47
  606.7 1.3 convert_element_type.47
  608.0 0.8 slice_bitcast_fusion
Async XLA Ops:
  7.2 78.2 %all-gather.4.cloned.1.call-start = ((), (), s32[]{:S(2)}) async-start(), calls=%async_computation.2 | async-start | bytes 4456448 | tf_op jit(solution)/shard_map/all_gather | solution.py:35
  7.9 247.1 %all-gather.6.cloned.1.call-start = ((), (), s32[]{:S(2)}) async-start(), calls=%async_computation.3 | async-start | bytes 8257536 | tf_op jit(solution)/shard_map/all_gather | solution.py:37
  8.6 398.1 %all-gather.8.cloned.1.call-start = ((), (), s32[]{:S(2)}) async-start(), calls=%async_computation.4 | async-start | bytes 8257536 | tf_op jit(solution)/shard_map/all_gather | solution.py:42
  14.4 258.7 %all-to-all-start = ((bf16[8,512,896]{2,1,0:T(8,128)(2,1)}), bf16[8,512,896]{2,1,0:T(8,128)(2,1)}, u32[]{:S(2)}, u32[]{:S(2)}) async-start(bf16[8,512,896]{2,1,0:T(8,128)(2,1)} %stack.8), calls=%async_computation | async-start | bytes 14680064 | tf_op jit(solution)/shard_map/all_to_all | solution.py:12
  20.4 586.3 %reduce-scatter.2.cloned.1.call-start = ((), (), s32[]{:S(2)}) async-start(), calls=%async_computation.5 | async-start | bytes 17825792 | tf_op jit(solution)/shard_map/reduce_scatter | solution.py:47
  255.0 10.2 %copy-start = (bf16[4096,896]{1,0:T(8,128)(2,1)S(1)}, bf16[4096,896]{1,0:T(8,128)(2,1)}, u32[]{:S(2)}) copy-start(bf16[4096,896]{1,0:T(8,128)(2,1)} %all-gather.6.cloned.1.call-done) | copy-start | bytes 22020100
  255.0 10.2 %copy-start.1 = (bf16[512,4096]{1,0:T(8,128)(2,1)S(1)}, bf16[512,4096]{1,0:T(8,128)(2,1)}, u32[]{:S(2)}) copy-start(bf16[512,4096]{1,0:T(8,128)(2,1)} %all-gather.4.cloned.1.call-done) | copy-start | bytes 12582916
Sparse Core Ops, SparseCore 0:
  10.3 75.0 all-gather.3
  87.0 167.9 all-gather.5
  256.6 150.0 all-gather.7
  458.5 148.1 reduce-scatter.1
